TPU v7x, 512 devices: a whole 4x4x16 slice. The times are simulated.
512 devices in a mesh: inp: 8 (over z_lo), out: 8 (over y, z_hi), tok: 8 (over x, core).
Axes of the slice: x: 4, y: 4, z: 16 (z_hi: 2, z_lo: 8; z = z_hi * 8 + z_lo), core: 2. Of those that a mesh axis runs over, the one named last changes fastest.
Arguments:
- saved_input: float32 [1024, 4096], P('tok', 'inp'), may hold values from -6 to 6
- saved_gate: float32 [1024, 28672], P('inp', ('out', 'tok')), may hold values from -6 to 6
- saved_up: float32 [1024, 28672], P('inp', ('out', 'tok')), may hold values from -6 to 6
- out_grad: bfloat16 [1024, 4096], P('tok', 'inp'), may hold values from -1.5 to 1.5
- w_gate: bfloat16 [4096, 28672], P('inp', ('out', 'tok')), may hold values from -0.09375 to 0.09375
- w_up: bfloat16 [4096, 28672], P('inp', ('out', 'tok')), may hold values from -0.09375 to 0.09375
- w_down: bfloat16 [28672, 4096], P(('out', 'tok'), 'inp'), may hold values from -0.03125 to 0.03125
Outputs:
- input_grad: bfloat16 [1024, 4096], P(('out', 'tok'), 'inp')
- gate_wgrad: bfloat16 [4096, 28672], P('inp', ('out', 'tok'))
- up_wgrad: bfloat16 [4096, 28672], P('inp', ('out', 'tok'))
- down_wgrad: bfloat16 [28672, 4096], P(('out', 'tok'), 'inp')
All inputs are finite; a program needn't handle non-finite values.
Results may differ from a plain program's by a relative error of at most 0.0057.
Values may be sent and summed in bfloat16 or wider, within the bound.
A program may use at most 64 MiB of HBM per device.

v0:
```python
import jax
import jax.numpy as jnp
from jax import lax
from jax.sharding import PartitionSpec as P


def local_terms(hidden_grad, gate_vals, up_vals):
    sig = jax.nn.sigmoid(gate_vals)
    hidden = (gate_vals * sig * up_vals).astype(jnp.bfloat16)
    gate_grad = (hidden_grad * up_vals * sig * (1.0 + gate_vals * (1.0 - sig))).astype(jnp.bfloat16)
    up_grad = (hidden_grad * gate_vals * sig).astype(jnp.bfloat16)
    return (gate_grad, up_grad, hidden)


def local(saved_input, saved_gate, saved_up, out_grad, w_gate, w_up, w_down):
    last_dims = (((1,), (1,)), ((), ()))
    lead_dims = (((0,), (0,)), ((), ()))
    input_b = saved_input.astype(jnp.bfloat16)
    all_inputs, all_grads = (
        lax.all_gather(input_b, "tok", axis=0, tiled=True),
        lax.all_gather(out_grad, "tok", axis=0, tiled=True),
    )
    partial_sum = lax.dot_general(all_grads, w_down, last_dims, preferred_element_type=jnp.float32)
    hidden_grad = lax.psum(partial_sum, "inp")
    gate_all, up_all = (
        lax.all_gather(saved_gate, "inp", axis=0, tiled=True),
        lax.all_gather(saved_up, "inp", axis=0, tiled=True),
    )
    gate_grad, up_grad, hidden = local_terms(hidden_grad, gate_all, up_all)
    gate_wgrad = lax.dot_general(
        all_inputs, gate_grad, lead_dims, preferred_element_type=jnp.float32
    ).astype(jnp.bfloat16)
    up_wgrad = lax.dot_general(
        all_inputs, up_grad, lead_dims, preferred_element_type=jnp.float32
    ).astype(jnp.bfloat16)
    down_wgrad = lax.dot_general(
        hidden, all_grads, lead_dims, preferred_element_type=jnp.float32
    ).astype(jnp.bfloat16)
    result = lax.dot_general(gate_grad, w_gate, last_dims, preferred_element_type=jnp.float32)
    summed = lax.psum_scatter(
        result + lax.dot_general(up_grad, w_up, last_dims, preferred_element_type=jnp.float32),
        ("out", "tok"),
        scatter_dimension=0,
        tiled=True,
    )
    return (summed.astype(jnp.bfloat16), gate_wgrad, up_wgrad, down_wgrad)


def solution(mesh):
    placed = (
        P("tok", "inp"),
        P("inp", ("out", "tok")),
        P("inp", ("out", "tok")),
        P("tok", "inp"),
        P("inp", ("out", "tok")),
        P("inp", ("out", "tok")),
        P(("out", "tok"), "inp"),
    )
    return jax.shard_map(
        local,
        mesh=mesh,
        in_specs=placed,
        out_specs=(
            P(("out", "tok"), "inp"),
            P("inp", ("out", "tok")),
            P("inp", ("out", "tok")),
            P(("out", "tok"), "inp"),
        ),
        check_vma=False,
    )
```

profile of v0, /device:TPU:32, one launch (start us, length us, event | category | flops | bytes accessed | tf_op | source)
XLA Modules:
  0.0 933.5 jit_solution(1426230124523403233)
XLA Ops:
  7.2 0.0 copy-start
  7.2 0.0 all-gather.5.cloned.1.call-start
  7.2 0.7 all-gather.5.cloned.1.call-update
  7.9 0.0 all-gather.7.cloned.1.call-start
  8.0 0.7 all-gather.7.cloned.1.call-update
  8.7 0.0 all-gather.9.cloned.1.call-start
  8.7 0.7 all-gather.9.cloned.1.call-update
  9.4 0.0 copy-start.3
  9.4 0.0 all-reduce.2.cloned.1.call-start
  9.5 35.9 %all-gather.5.cloned.1.call-done = bf16[1024,512]{1,0:T(8,128)(2,1)} async-done(((bf16[128,512]{1,0:T(8,128)(2,1)}), bf16[1024,512]{1,0:T(8,128)(2,1)}) %all-gather.5.cloned.1.call-update) | async-done | bytes 1048592 | tf_op jit(solution)/shard_map/all_gather | solution.py:21
  45.3 3.3 fusion.3
  48.6 0.0 all-reduce.2.cloned.1.call-update
  48.7 0.0 all-gather.11.cloned.1.call-start
  48.7 0.0 copy-done.3
  48.7 0.7 convert_element_type.33
  49.4 0.0 all-gather.11.cloned.1.call-update
  49.4 0.0 reduce-scatter.2.cloned.1.call-start
  49.5 62.5 %all-gather.7.cloned.1.call-done = f32[1024,448]{0,1:T(8,128)} async-done(((f32[128,448]{0,1:T(8,128)}), f32[1024,448]{0,1:T(8,128)}) %all-gather.7.cloned.1.call-update) | async-done | bytes 1835024 | tf_op jit(solution)/shard_map/all_gather | solution.py:27
  112.0 67.4 %all-gather.9.cloned.1.call-done = f32[1024,448]{0,1:T(8,128)} async-done(((f32[128,448]{0,1:T(8,128)}), f32[1024,448]{0,1:T(8,128)}) %all-gather.9.cloned.1.call-update) | async-done | bytes 1835024 | tf_op jit(solution)/shard_map/all_gather | solution.py:26
  179.4 135.5 %all-reduce.2.cloned.1.call-done = f32[1024,448]{0,1:T(8,128)} async-done(((f32[1024,448]{0,1:T(8,128)}), f32[1024,448]{0,1:T(8,128)}) %all-reduce.2.cloned.1.call-update) | async-done | bytes 1835024 | tf_op jit(solution)/shard_map/psum | solution.py:24
  314.8 3.7 multiply_convert_fusion.1
  318.5 0.0 copy-start.2
  318.6 0.0 copy-done
  318.6 0.7 fusion.4
  319.3 0.2 copy-done.2
  319.6 2.1 convolution_add_fusion
  321.6 0.0 copy-start.1
  321.6 0.0 reduce-scatter.2.cloned.1.call-update
  321.6 1.2 copy-done.1
  322.8 3.5 convolution_convert_fusion
  326.3 22.1 %all-gather.11.cloned.1.call-done = bf16[1024,512]{1,0:T(8,128)(2,1)} async-done(((bf16[128,512]{1,0:T(8,128)(2,1)}), bf16[1024,512]{1,0:T(8,128)(2,1)}) %all-gather.11.cloned.1.call-update) | async-done | bytes 1048592 | tf_op jit(solution)/shard_map/all_gather | solution.py:20
  348.4 0.0 copy-start.4
  348.4 2.7 fusion
  351.1 0.0 copy-done.4
  351.1 1.4 fusion.1
  352.5 572.8 %reduce-scatter.2.cloned.1.call-done = f32[16,512]{1,0:T(8,128)} async-done(((f32[1024,512]{1,0:T(8,128)}), f32[16,512]{1,0:T(8,128)}) %reduce-scatter.2.cloned.1.call-update) | async-done | bytes 32784 | tf_op jit(solution)/shard_map/reduce_scatter | solution.py:40
  925.3 1.4 convert_element_type.32
Async XLA Ops:
  7.2 311.4 %copy-start = (bf16[512,448]{0,1:T(8,128)(2,1)S(1)}, bf16[512,448]{0,1:T(8,128)(2,1)}, u32[]{:S(2)}) copy-start(bf16[512,448]{0,1:T(8,128)(2,1)} %param.11) | copy-start | bytes 1376260
  7.2 38.1 %all-gather.5.cloned.1.call-start = ((), (), s32[]{:S(2)}) async-start(), calls=%async_computation.1 | async-start | bytes 1179648 | tf_op jit(solution)/shard_map/all_gather | solution.py:21
  7.9 104.1 %all-gather.7.cloned.1.call-start = ((), (), s32[]{:S(2)}) async-start(), calls=%async_computation.3 | async-start | bytes 2064384 | tf_op jit(solution)/shard_map/all_gather | solution.py:27
  8.7 170.7 %all-gather.9.cloned.1.call-start = ((), (), s32[]{:S(2)}) async-start(), calls=%async_computation.4 | async-start | bytes 2064384 | tf_op jit(solution)/shard_map/all_gather | solution.py:26
  9.4 39.3 %copy-start.3 = (f32[128,512]{1,0:T(8,128)S(1)}, f32[128,512]{1,0:T(8,128)}, u32[]{:S(2)}) copy-start(f32[128,512]{1,0:T(8,128)} %param.7) | copy-start | bytes 786436
  9.4 305.4 %all-reduce.2.cloned.1.call-start = ((), (), s32[]{:S(2)}) async-start(), calls=%async_computation.2 | async-start | bytes 3670016 | tf_op jit(solution)/shard_map/psum | solution.py:24
  48.7 299.7 %all-gather.11.cloned.1.call-start = ((), (), s32[]{:S(2)}) async-start(), calls=%async_computation.6 | async-start | bytes 1179648 | tf_op jit(solution)/shard_map/all_gather | solution.py:20
  49.4 875.9 %reduce-scatter.2.cloned.1.call-start = ((), (), s32[]{:S(2)}) async-start(), calls=%async_computation.5 | async-start | bytes 2129920 | tf_op jit(solution)/shard_map/reduce_scatter | solution.py:40
  318.5 1.0 copy-start.2
  321.6 1.2 copy-start.1
  348.4 2.7 copy-start.4
Sparse Core Ops, SparseCore 0:
  10.2 35.1 all-gather.4
  47.3 64.6 all-gather.6
  114.0 65.3 all-gather.8
  182.2 132.6 all-reduce.1
  317.4 30.9 all-gather.10
  351.0 574.1 reduce-scatter.1
where the time goes:
time: 934 us; the launch traced here: 933 us
  waiting for transfers between devices  898 us (96%)
  between operations  14.2 us (2%)
  matrix products  13.7 us (1%)
    reduce_scatter x1, waiting for transfers between devices, local(): lax.psum_scatter(result + lax.dot_general(up_grad, w_up, last_dims, prefe...  573 us
    psum x1, waiting for transfers between devices, local(): hidden_grad = lax.psum(partial_sum, 'inp')  135 us
    all_gather x1, waiting for transfers between devices, local(): lax.all_gather(saved_gate, 'inp', axis=0, tiled=True)  67.4 us
    all_gather x1, waiting for transfers between devices, local(): lax.all_gather(saved_up, 'inp', axis=0, tiled=True)  62.5 us
    all_gather x1, waiting for transfers between devices, local(): lax.all_gather(out_grad, 'tok', axis=0, tiled=True)  35.9 us
    all_gather x1, waiting for transfers between devices, local(): lax.all_gather(input_b, 'tok', axis=0, tiled=True)  22.1 us
  transfers between devices with their start and end apart: 6, of which 6 were waited for; matrix products, arithmetic and copies ran while one was open for 2% of the time, Pallas kernels for 0%

commit v1 on v0

--- a/solution.py
+++ b/solution.py
@@ -16,17 +16,14 @@
     last_dims = (((1,), (1,)), ((), ()))
     lead_dims = (((0,), (0,)), ((), ()))
     input_b = saved_input.astype(jnp.bfloat16)
-    all_inputs, all_grads = (
-        lax.all_gather(input_b, "tok", axis=0, tiled=True),
-        lax.all_gather(out_grad, "tok", axis=0, tiled=True),
-    )
+    all_grads = lax.all_gather(out_grad, "tok", axis=0, tiled=True)
+    all_inputs = lax.all_gather(input_b, "tok", axis=0, tiled=True)
     partial_sum = lax.dot_general(all_grads, w_down, last_dims, preferred_element_type=jnp.float32)
-    hidden_grad = lax.psum(partial_sum, "inp")
-    gate_all, up_all = (
-        lax.all_gather(saved_gate, "inp", axis=0, tiled=True),
-        lax.all_gather(saved_up, "inp", axis=0, tiled=True),
-    )
-    gate_grad, up_grad, hidden = local_terms(hidden_grad, gate_all, up_all)
+    hidden_grad = lax.psum_scatter(partial_sum, "inp", scatter_dimension=0, tiled=True)
+    gate_grad, up_grad, hidden = local_terms(hidden_grad, saved_gate, saved_up)
+    gate_grad = lax.all_gather(gate_grad, "inp", axis=0, tiled=True)
+    up_grad = lax.all_gather(up_grad, "inp", axis=0, tiled=True)
+    hidden = lax.all_gather(hidden, "inp", axis=0, tiled=True)
     gate_wgrad = lax.dot_general(
         all_inputs, gate_grad, lead_dims, preferred_element_type=jnp.float32
     ).astype(jnp.bfloat16)
@@ -37,12 +34,13 @@
         hidden, all_grads, lead_dims, preferred_element_type=jnp.float32
     ).astype(jnp.bfloat16)
     result = lax.dot_general(gate_grad, w_gate, last_dims, preferred_element_type=jnp.float32)
-    summed = lax.psum_scatter(
-        result + lax.dot_general(up_grad, w_up, last_dims, preferred_element_type=jnp.float32),
-        ("out", "tok"),
-        scatter_dimension=0,
-        tiled=True,
-    )
+    result = result + lax.dot_general(up_grad, w_up, last_dims, preferred_element_type=jnp.float32)
+    tokens, width = result.shape
+    outs, toks = lax.axis_size("out"), lax.axis_size("tok")
+    rows = tokens // (outs * toks)
+    result = result.reshape(outs, toks, rows, width).transpose(1, 0, 2, 3).reshape(tokens, width)
+    summed = lax.psum_scatter(result, "tok", scatter_dimension=0, tiled=True)
+    summed = lax.psum_scatter(summed, "out", scatter_dimension=0, tiled=True)
     return (summed.astype(jnp.bfloat16), gate_wgrad, up_wgrad, down_wgrad)
 
 

time: 934 us -> 379 us (0.41)
  the two profiles are of different devices: /device:TPU:32 before, /device:TPU:24 now
where the time goes in v1:
time: 379 us; the launch traced here: 378 us
  waiting for transfers between devices  209 us (55%)
  blocking collectives  138 us (36%)
  between operations  13.8 us (4%)
  matrix products  11.4 us (3%)
    reduce_scatter x1, waiting for transfers between devices, local(): summed = lax.psum_scatter(summed, 'out', scatter_dimension=0, tiled=True)  100 us
    reduce_scatter x1, waiting for transfers between devices, local(): lax.psum_scatter(partial_sum, 'inp', scatter_dimension=0, tiled=True)  71.1 us
    all_gather x1, blocking collectives, local(): up_grad = lax.all_gather(up_grad, 'inp', axis=0, tiled=True)  47.1 us
    all_gather x1, blocking collectives, local(): hidden = lax.all_gather(hidden, 'inp', axis=0, tiled=True)  45.6 us
    all_gather x1, blocking collectives, local(): gate_grad = lax.all_gather(gate_grad, 'inp', axis=0, tiled=True)  45.5 us
    all_gather x1, waiting for transfers between devices, local(): all_grads = lax.all_gather(out_grad, 'tok', axis=0, tiled=True)  37.4 us
  transfers between devices with their start and end apart: 5, of which 3 were waited for; matrix products, arithmetic and copies ran while one was open for 3% of the time, Pallas kernels for 0%

profile of v1, /device:TPU:24, one launch (start us, length us, event | category | flops | bytes accessed | tf_op | source)
XLA Modules:
  0.0 377.7 jit_solution(17692691491800857276)
XLA Ops:
  7.2 0.0 copy-start
  7.2 0.0 all-gather.3.cloned.1.call-start
  7.2 0.7 all-gather.3.cloned.1.call-update
  7.9 0.0 copy-start.3
  7.9 0.0 copy-start.4
  7.9 0.0 copy-start.5
  7.9 0.0 reduce-scatter.4.cloned.1.call-start
  8.0 37.4 %all-gather.3.cloned.1.call-done = bf16[1024,512]{1,0:T(8,128)(2,1)} async-done(((bf16[128,512]{1,0:T(8,128)(2,1)}), bf16[1024,512]{1,0:T(8,128)(2,1)}) %all-gather.3.cloned.1.call-update) | async-done | bytes 1048592 | tf_op jit(solution)/shard_map/all_gather | solution.py:19
  45.4 3.3 fusion.2
  48.7 0.0 reduce-scatter.4.cloned.1.call-update
  48.7 0.0 all-gather.5.cloned.1.call-start
  48.8 0.0 copy-done.3
  48.8 0.7 convert_element_type.33
  49.4 0.0 all-gather.5.cloned.1.call-update
  49.5 0.0 reduce-scatter.6.cloned.1.call-start
  49.5 71.1 %reduce-scatter.4.cloned.1.call-done = f32[128,448]{0,1:T(8,128)} async-done(((f32[1024,448]{0,1:T(8,128)}), f32[128,448]{0,1:T(8,128)}) %reduce-scatter.4.cloned.1.call-update) | async-done | bytes 229392 | tf_op jit(solution)/shard_map/reduce_scatter | solution.py:22
  120.6 0.0 copy-done.4
  120.6 0.0 copy-done.5
  120.6 1.1 multiply_convert_fusion
  121.7 45.5 %all_gather.16 = bf16[1024,448]{0,1:T(8,128)(2,1)S(1)} all-gather(bf16[128,448]{0,1:T(8,128)(2,1)S(1)} %get-tuple-element.5), channel_id=1, replica_groups=mesh['inp'=8,'out'=8,'tok'=8] {'inp'}, dimensions={0}, use_global_device_ids=true | all-gather | bytes 1032192 | tf_op jit(solution)/shard_map/all_gather | solution.py:24
  167.2 0.0 copy-done
  167.2 0.0 copy-start.2
  167.2 0.7 fusion.3
  167.9 47.1 %all_gather.17 = bf16[1024,448]{0,1:T(8,128)(2,1)S(1)} all-gather(bf16[128,448]{0,1:T(8,128)(2,1)S(1)} %get-tuple-element.6), channel_id=1, replica_groups=mesh['inp'=8,'out'=8,'tok'=8] {'inp'}, dimensions={0}, use_global_device_ids=true | all-gather | bytes 1032192 | tf_op jit(solution)/shard_map/all_gather | solution.py:25
  215.0 0.0 copy-done.2
  215.0 0.8 convolution_add_fusion
  215.7 1.6 copy.11
  217.3 0.0 reduce-scatter.6.cloned.1.call-update
  217.3 0.0 reduce-scatter.8.cloned.1.call-start
  217.4 0.0 all-gather.5.cloned.1.call-done
  217.4 2.6 fusion
  220.1 0.0 copy-start.1
  220.1 45.6 %all_gather.19 = bf16[1024,448]{0,1:T(8,128)(2,1)S(1)} all-gather(bf16[128,448]{0,1:T(8,128)(2,1)S(1)} %get-tuple-element.4), channel_id=1, replica_groups=mesh['inp'=8,'out'=8,'tok'=8] {'inp'}, dimensions={0}, use_global_device_ids=true | all-gather | bytes 1032192 | tf_op jit(solution)/shard_map/all_gather | solution.py:26
  265.6 0.0 reduce-scatter.6.cloned.1.call-done
  265.6 0.0 reduce-scatter.8.cloned.1.call-update
  265.6 2.6 fusion.1
  268.3 0.0 copy-done.1
  268.3 1.4 convolution_convert_fusion
  269.7 100.1 %reduce-scatter.8.cloned.1.call-done = f32[16,512]{1,0:T(8,128)} async-done(((f32[128,512]{1,0:T(8,128)}), f32[16,512]{1,0:T(8,128)}) %reduce-scatter.8.cloned.1.call-update) | async-done | bytes 32784 | tf_op jit(solution)/shard_map/reduce_scatter | solution.py:43
  369.8 1.4 convert_element_type.32
Async XLA Ops:
  7.2 160.0 %copy-start = (bf16[512,448]{0,1:T(8,128)(2,1)S(1)}, bf16[512,448]{0,1:T(8,128)(2,1)}, u32[]{:S(2)}) copy-start(bf16[512,448]{0,1:T(8,128)(2,1)} %param.11) | copy-start | bytes 1376260
  7.2 38.2 %all-gather.3.cloned.1.call-start = ((), (), s32[]{:S(2)}) async-start(), calls=%async_computation.3 | async-start | bytes 1179648 | tf_op jit(solution)/shard_map/all_gather | solution.py:19
  7.9 40.8 %copy-start.3 = (f32[128,512]{1,0:T(8,128)S(1)}, f32[128,512]{1,0:T(8,128)}, u32[]{:S(2)}) copy-start(f32[128,512]{1,0:T(8,128)} %param.7) | copy-start | bytes 786436
  7.9 112.7 %copy-start.4 = (f32[128,448]{0,1:T(8,128)S(1)}, f32[128,448]{0,1:T(8,128)}, u32[]{:S(2)}) copy-start(f32[128,448]{0,1:T(8,128)} %param.9) | copy-start | bytes 688132
  7.9 112.7 %copy-start.5 = (f32[128,448]{0,1:T(8,128)S(1)}, f32[128,448]{0,1:T(8,128)}, u32[]{:S(2)}) copy-start(f32[128,448]{0,1:T(8,128)} %param.8) | copy-start | bytes 688132
  7.9 112.7 %reduce-scatter.4.cloned.1.call-start = ((), (), s32[]{:S(2)}) async-start(), calls=%async_computation.4 | async-start | bytes 2064384 | tf_op jit(solution)/shard_map/reduce_scatter | solution.py:22
  48.7 168.7 %all-gather.5.cloned.1.call-start = ((), (), s32[]{:S(2)}) async-start(), calls=%async_computation.7 | async-start | bytes 1179648 | tf_op jit(solution)/shard_map/all_gather | solution.py:20
  49.5 216.2 %reduce-scatter.6.cloned.1.call-start = ((), (), s32[]{:S(2)}) async-start(), calls=%async_computation.5 | async-start | bytes 2359296 | tf_op jit(solution)/shard_map/reduce_scatter | solution.py:42
  167.2 47.8 %copy-start.2 = (bf16[512,448]{0,1:T(8,128)(2,1)S(1)}, bf16[512,448]{0,1:T(8,128)(2,1)}, u32[]{:S(2)}) copy-start(bf16[512,448]{0,1:T(8,128)(2,1)} %param.12) | copy-start | bytes 1376260
  217.3 152.4 %reduce-scatter.8.cloned.1.call-start = ((), (), s32[]{:S(2)}) async-start(), calls=%async_computation.6 | async-start | bytes 294912 | tf_op jit(solution)/shard_map/reduce_scatter | solution.py:43
  220.1 48.2 %copy-start.1 = (bf16[1024,512]{1,0:T(8,128)(2,1)S(1)}, bf16[1024,512]{1,0:T(8,128)(2,1)}, u32[]{:S(2)}) copy-start(bf16[1024,512]{1,0:T(8,128)(2,1)} %all-gather.3.cloned.1.call-done) | copy-start | bytes 3145732
Sparse Core Ops, SparseCore 0:
  10.2 35.1 all-gather.2
  48.8 71.7 reduce-scatter.3
  123.4 25.8 all-gather.4
  217.5 36.2 reduce-scatter.5
  265.8 103.9 reduce-scatter.7

commit v2 on v1

v2 whole, which is shorter than its diff:
```python
import functools

import jax
import jax.numpy as jnp
from jax import lax
from jax.experimental import pallas as pl
from jax.experimental.pallas import tpu as pltpu
from jax.sharding import PartitionSpec as P

MESH = pl.DeviceIdType.MESH
F32 = jnp.float32
BF16 = jnp.bfloat16
LAST = (((1,), (1,)), ((), ()))
LEAD = (((0,), (0,)), ((), ()))
NC = 2
NZ = 2


def dot(a, b, dims=(((1,), (0,)), ((), ()))):
    return lax.dot_general(a, b, dims, preferred_element_type=F32)


def kernel(
    sizes,
    x_ref, g_ref, u_ref, go_ref, wg_ref, wu_ref, wd_ref,
    ig_ref, gw_ref, uw_ref, dw_ref,
    GA, XA, GU, H, RU, RD, PS, TA, TB, GW, UW, DW, IG2, IGR, XS, XR, YS, YR, ZR,
    ga_s, ga_r, xa_s, xa_r, gu_s, gu_r, h_s, h_r, ru_s, ru_r, rd_s, rd_r,
    ig_s, ig_r, xs_s, xs_r, ys_s, ys_r, z_s, z_r,
):
    NI, NO, NT = sizes
    NX, NY = NT // NC, NO // NZ
    zi, o, t = lax.axis_index("inp"), lax.axis_index("out"), lax.axis_index("tok")
    x, core = t // NC, t % NC
    y, zh = o // NZ, o % NZ
    F, tb = g_ref.shape
    ts, D = go_ref.shape
    rows = tb // NT

    def at_inp(k):
        return {"inp": k}

    def at_tok(k):
        return {"tok": k}

    def at_out(k):
        return {"out": k}

    def rc(src, dst, ss, rs, dev):
        return pltpu.make_async_remote_copy(
            src_ref=src, dst_ref=dst, send_sem=ss, recv_sem=rs, device_id=dev, device_id_type=MESH
        )

    has_up, has_dn = zi < NI - 1, zi > 0
    sib = x * NC + (1 - core)

    def tok_of(dx):
        return ((x + dx + NX) % NX) * NC + core

    barrier = pltpu.get_barrier_semaphore()

    def greet(dev):
        pl.semaphore_signal(barrier, inc=1, device_id=dev, device_id_type=MESH)

    greet(at_tok(sib))
    for dx in range(1, NX):
        greet(at_tok(tok_of(dx)))
    for dy in range(1, NY):
        greet(at_out(((y + dy) % NY) * NZ + zh))
    greet(at_out(y * NZ + 1 - zh))
    pl.when(has_up)(lambda: greet(at_inp(zi + 1)))
    pl.when(has_dn)(lambda: greet(at_inp(zi - 1)))
    ends = jnp.where(has_up, 1, 0) + jnp.where(has_dn, 1, 0)
    pl.semaphore_wait(barrier, 1 + (NX - 1) + (NY - 1) + 1 + ends)

    def gather_tok(buf, ss, rs):
        def shard(k):
            return buf.at[pl.ds(pl.multiple_of(k * ts, ts), ts)]

        def copy(k, slot, dev):
            return rc(shard(k), shard(k), ss.at[slot], rs.at[k], dev)

        sends = [copy(t, 0, at_tok(sib))]
        near = []
        if NX > 1:
            near.append(1)
        if NX > 2:
            near.append(-1)
        for i, dx in enumerate(near):
            sends.append(copy(t, 1 + i, at_tok(tok_of(dx))))

        def begin():
            for c in sends:
                c.start()

        def middle():
            slot = 3
            for dx in near:
                k = tok_of(dx)
                copy(k, 0, at_tok(sib)).wait_recv()
                c = copy(k, slot, at_tok(sib))
                c.start()
                sends.append(c)
                slot += 1
            if NX > 2:
                c = copy(tok_of(2 * core - 1), slot, at_tok(tok_of(1 - 2 * core)))
                c.start()
                sends.append(c)

        def end():
            if NX > 2:
                k = tok_of(2)
                copy(k, 0, at_tok(sib)).wait_recv()
                c = copy(k, 6, at_tok(sib))
                c.start()
                sends.append(c)
            for dx in range(NX):
                k = ((x + dx) % NX) * NC + 1 - core
                copy(k, 0, at_tok(sib)).wait_recv()

        def drain():
            for c in sends:
                c.wait_send()

        return begin, middle, end, drain

    def hand(buf, ss, rs, j, up):
        return rc(buf.at[j], buf.at[j], ss.at[up, j], rs.at[j], at_inp(zi + 1 if up else zi - 1))

    def own_both(buf, ss, rs):
        pl.when(has_up)(lambda: hand(buf, ss, rs, zi, 1).start())
        pl.when(has_dn)(lambda: hand(buf, ss, rs, zi, 0).start())

    def pass_on(buf, ss, rs, s):
        @pl.when(zi + s <= NI - 1)
        def _():
            hand(buf, ss, rs, zi + s, 1).wait_recv()
            pl.when(has_dn)(lambda: hand(buf, ss, rs, zi + s, 0).start())

        @pl.when(zi - s >= 0)
        def _():
            hand(buf, ss, rs, zi - s, 0).wait_recv()
            pl.when(has_up)(lambda: hand(buf, ss, rs, zi - s, 1).start())

    def drain_z(buf, ss, rs):
        def body(j, carry):
            pl.when(jnp.logical_and(has_up, j <= zi))(lambda: hand(buf, ss, rs, j, 1).wait_send())
            pl.when(jnp.logical_and(has_dn, j >= zi))(lambda: hand(buf, ss, rs, j, 0).wait_send())
            return carry

        lax.fori_loop(0, NI, body, 0)

    def order(n):
        m = jnp.minimum(zi, NI - 1 - zi)
        half = (n + 1) // 2
        near = jnp.where(n % 2 == 1, zi + half, zi - half)
        far = jnp.where(zi <= m, n, NI - 1 - n)
        return jnp.where(n <= 2 * m, near, far)

    def block(buf, j):
        return buf[pl.ds(pl.multiple_of(j * tb, tb), tb), :]

    def chain(buf, ss, rs, d, up):
        return rc(buf.at[d], buf.at[d], ss.at[d], rs.at[d], at_inp(zi + 1 if up else zi - 1))

    def slot(k):
        @pl.when(jnp.logical_and(zi <= k, has_up))
        def _():
            d = NI - 1 - k + zi
            PS[...] = dot(wd_ref[...], block(GA, d), LAST)

            @pl.when(has_dn)
            def _():
                chain(RU, ru_s, ru_r, d, 1).wait_recv()
                PS[...] += RU[d].astype(F32)

            RU[d] = PS[...].astype(BF16)
            chain(RU, ru_s, ru_r, d, 1).start()

        @pl.when(jnp.logical_and(k >= NI - 1 - zi, has_dn))
        def _():
            d = k - (NI - 1 - zi)
            PS[...] = dot(wd_ref[...], block(GA, d), LAST)

            @pl.when(has_up)
            def _():
                chain(RD, rd_s, rd_r, d, 0).wait_recv()
                PS[...] += RD[d].astype(F32)

            RD[d] = PS[...].astype(BF16)
            chain(RD, rd_s, rd_r, d, 0).start()

    def close_chains():
        PS[...] = dot(wd_ref[...], block(GA, zi), LAST)

        @pl.when(has_dn)
        def _():
            chain(RU, ru_s, ru_r, zi, 1).wait_recv()
            PS[...] += RU[zi].astype(F32)

        @pl.when(has_up)
        def _():
            chain(RD, rd_s, rd_r, zi, 0).wait_recv()
            PS[...] += RD[zi].astype(F32)

        H[zi] = PS[...].astype(BF16)

    def drain_chains():
        def body(d, carry):
            pl.when(jnp.logical_and(has_up, d > zi))(lambda: chain(RU, ru_s, ru_r, d, 1).wait_send())
            pl.when(jnp.logical_and(has_dn, d < zi))(lambda: chain(RD, rd_s, rd_r, d, 0).wait_send())
            return carry

        lax.fori_loop(0, NI, body, 0)

    def terms(n, first):
        j = order(n)
        g, u = GU[j, 0].astype(F32), GU[j, 1].astype(F32)
        sig = 1.0 / (1.0 + jnp.exp(-g))
        gs = g * sig
        TA[n] = u * sig * (1.0 + g * (1.0 - sig))
        TB[n] = gs
        part = dot((gs * u).astype(BF16), block(GA, j))
        if first:
            DW[...] = part
        else:
            DW[...] += part

    def grads(n):
        j = order(n)
        h = H[j].astype(F32)
        gg, ug = (h * TA[n]).astype(BF16), (h * TB[n]).astype(BF16)
        xb = block(XA, j)
        GW[...] += dot(gg, xb)
        UW[...] += dot(ug, xb)
        part = dot(gg, wg_ref[...], LEAD) + dot(ug, wu_ref[...], LEAD)
        part = part.reshape(NX, NC, rows, D)
        for c in range(NC):
            IG2[c, n] = part[:, c]
        ig_core(n).start()

    def ig_core(n):
        return rc(IG2.at[1 - core, n], IGR.at[n], ig_s.at[n], ig_r.at[n], at_tok(sib))

    def ig_x(n, dx):
        return rc(
            XS.at[n, (x + dx) % NX], XR.at[dx - 1, n], xs_s.at[dx - 1, n], xs_r.at[dx - 1, n], at_tok(tok_of(dx))
        )

    def ig_y(dy):
        yd = (y + dy) % NY
        return rc(
            YS.at[pl.ds(yd * NZ, NZ)], YR.at[dy - 1], ys_s.at[dy - 1], ys_r.at[dy - 1], at_out(yd * NZ + zh)
        )

    def sum_core(n):
        ig_core(n).wait()
        XS[n] = IG2[core, n] + IGR[n]
        for dx in range(1, NX):
            ig_x(n, dx).start()

    def sum_x(n):
        total = XS[n, x]
        for dx in range(1, NX):
            ig_x(n, dx).wait()
            total = total + XR[dx - 1, n]
        YS[order(n)] = total

    GA[pl.ds(pl.multiple_of(t * ts, ts), ts), :] = go_ref[...]
    g_begin, g_middle, g_end, g_drain = gather_tok(GA, ga_s, ga_r)
    g_begin()
    GU[zi, 0] = g_ref[...].astype(BF16)
    GU[zi, 1] = u_ref[...].astype(BF16)
    own_both(GU, gu_s, gu_r)
    XA[pl.ds(pl.multiple_of(t * ts, ts), ts), :] = x_ref[...].astype(BF16)
    x_begin, x_middle, x_end, x_drain = gather_tok(XA, xa_s, xa_r)
    g_middle()
    x_begin()
    g_end()
    done_gu = done_terms = 0

    def gu_step():
        nonlocal done_gu
        done_gu += 1
        pass_on(GU, gu_s, gu_r, done_gu)

    def some_terms():
        nonlocal done_terms
        terms(done_terms, done_terms == 0)
        done_terms += 1

    for k in range(NI - 1):
        slot(k)
        want = (k + 1) * 5 // 7
        while done_gu < want:
            gu_step()
        if k == 0:
            x_middle()
        if k == 1:
            x_end()
        if k >= 1 and done_terms <= done_gu:
            some_terms()
    if NI == 2:
        x_end()
    close_chains()
    own_both(H, h_s, h_r)
    while done_gu < NI - 1:
        gu_step()
    while done_terms < NI:
        some_terms()
    GW[...] = jnp.zeros_like(GW)
    UW[...] = jnp.zeros_like(UW)
    grads(0)

    def h_step(s, carry):
        pass_on(H, h_s, h_r, s)
        grads(s)
        sum_core(s - 1)
        pl.when(s >= 2)(lambda: sum_x(s - 2))
        return carry

    lax.fori_loop(1, NI, h_step, 0)
    sum_core(NI - 1)
    sum_x(NI - 2)
    gw_ref[...] = GW[...].astype(BF16)
    uw_ref[...] = UW[...].astype(BF16)
    sum_x(NI - 1)
    for dy in range(1, NY):
        ig_y(dy).start()
    dw_ref[...] = DW[...].astype(BF16)
    total = YS[pl.ds(y * NZ, NZ)]
    for dy in range(1, NY):
        ig_y(dy).wait()
        total = total + YR[dy - 1]
    YS[pl.ds(y * NZ, NZ)] = total
    last = rc(YS.at[y * NZ + 1 - zh], ZR, z_s, z_r, at_out(y * NZ + 1 - zh))
    last.start()
    g_drain()
    x_drain()
    drain_z(GU, gu_s, gu_r)
    drain_z(H, h_s, h_r)
    drain_chains()
    last.wait()
    ig_ref[...] = (YS[o] + ZR[...]).astype(BF16)


def local(saved_input, saved_gate, saved_up, out_grad, w_gate, w_up, w_down):
    sizes = tuple(lax.axis_size(a) for a in ("inp", "out", "tok"))
    NI, NO, NT = sizes
    NX, NY = NT // NC, NO // NZ
    ts, D = saved_input.shape
    tb, F = saved_gate.shape
    T = tb * NI
    rows = tb // NT
    dma = pltpu.SemaphoreType.DMA
    vmem = pl.BlockSpec(memory_space=pltpu.VMEM)
    ig, gw, uw, dw = pl.pallas_call(
        functools.partial(kernel, sizes),
        out_shape=(
            jax.ShapeDtypeStruct((rows, D), BF16),
            jax.ShapeDtypeStruct((F, D), BF16),
            jax.ShapeDtypeStruct((F, D), BF16),
            jax.ShapeDtypeStruct((F, D), BF16),
        ),
        in_specs=[vmem] * 7,
        out_specs=(vmem,) * 4,
        scratch_shapes=[
            pltpu.VMEM((T, D), BF16),
            pltpu.VMEM((T, D), BF16),
            pltpu.VMEM((NI, 2, F, tb), BF16),
            pltpu.VMEM((NI, F, tb), BF16),
            pltpu.VMEM((NI, F, tb), BF16),
            pltpu.VMEM((NI, F, tb), BF16),
            pltpu.VMEM((F, tb), F32),
            pltpu.VMEM((NI, F, tb), F32),
            pltpu.VMEM((NI, F, tb), F32),
            pltpu.VMEM((F, D), F32),
            pltpu.VMEM((F, D), F32),
            pltpu.VMEM((F, D), F32),
            pltpu.VMEM((NC, NI, NX, rows, D), F32),
            pltpu.VMEM((NI, NX, rows, D), F32),
            pltpu.VMEM((NI, NX, rows, D), F32),
            pltpu.VMEM((max(NX - 1, 1), NI, rows, D), F32),
            pltpu.VMEM((NO, rows, D), F32),
            pltpu.VMEM((max(NY - 1, 1), NZ, rows, D), F32),
            pltpu.VMEM((rows, D), F32),
            dma((7,)), dma((NT,)), dma((7,)), dma((NT,)),
            dma((2, NI)), dma((NI,)), dma((2, NI)), dma((NI,)),
            dma((NI,)), dma((NI,)), dma((NI,)), dma((NI,)),
            dma((NI,)), dma((NI,)),
            dma((max(NX - 1, 1), NI)), dma((max(NX - 1, 1), NI)),
            dma((max(NY - 1, 1),)), dma((max(NY - 1, 1),)), dma, dma,
        ],
        compiler_params=pltpu.CompilerParams(
            collective_id=0, has_side_effects=True, vmem_limit_bytes=56 * 1024 * 1024
        ),
    )(saved_input, saved_gate.T, saved_up.T, out_grad, w_gate.T, w_up.T, w_down)
    return ig, gw.T, uw.T, dw


def solution(mesh):
    placed = (
        P("tok", "inp"),
        P("inp", ("out", "tok")),
        P("inp", ("out", "tok")),
        P("tok", "inp"),
        P("inp", ("out", "tok")),
        P("inp", ("out", "tok")),
        P(("out", "tok"), "inp"),
    )
    return jax.shard_map(
        local,
        mesh=mesh,
        in_specs=placed,
        out_specs=(
            P(("out", "tok"), "inp"),
            P("inp", ("out", "tok")),
            P("inp", ("out", "tok")),
            P(("out", "tok"), "inp"),
        ),
        check_vma=False,
    )
```

time: 379 us -> 124 us (0.33)
  waiting for transfers between devices: 209 us -> 0 us
  blocking collectives: 138 us -> 0 us
  Pallas kernels: 0 us -> 116 us
  between operations: 13.8 us -> 0.64 us
  matrix products: 11.4 us -> 0 us
    reduce_scatter x3 -> x0, waiting for transfers between devices: 171 us -> none  [the longest x1 100 us: local(): summed = lax.psum_scatter(summed, 'out', scatter_dimension=0, tiled=True)]
    all_gather x3 -> x0, blocking collectives: 138 us -> none  [the longest x1 47.1 us: local(): up_grad = lax.all_gather(up_grad, 'inp', axis=0, tiled=True)]
    pallas_call x0 -> x1, Pallas kernels: none -> 116 us  [local(): pl.pallas_call(functools.partial(kernel, sizes), out_shape=(jax.ShapeDtyp...]
    all_gather x2 -> x0, waiting for transfers between devices: 37.4 us -> none  [the longest x1 37.4 us: local(): all_grads = lax.all_gather(out_grad, 'tok', axis=0, tiled=True)]
    dot_general x6 -> x0, matrix products: 11.4 us -> none  [the longest x1 3.27 us: local(): lax.dot_general(all_grads, w_down, last_dims, preferred_element_type=jnp....]
    unnamed x12 -> x8, local copies, waits for them, and re-layouts: 0.03 us -> 5.15 us
  transfers between devices with their start and end apart: 5 -> 0, of which waited for: 3 -> 0; matrix products, arithmetic and copies ran while one was open for 3% -> 0% of each run, Pallas kernels for 0% -> 0%
where the time goes in v2:
time: 124 us; the launch traced here: 122 us
  Pallas kernels  116 us (94%)
  local copies, waits for them, and re-layouts  5.15 us (4%)
    pallas_call x1, Pallas kernels, local(): pl.pallas_call(functools.partial(kernel, sizes), out_shape=(jax.ShapeDtyp...  116 us
    unnamed x8, local copies, waits for them, and re-layouts  5.15 us

profile of v2, /device:TPU:24, one launch (start us, length us, event | category | flops | bytes accessed | tf_op | source)
XLA Modules:
  0.0 121.9 jit_solution(391800290556149722)
XLA Ops:
  0.6 116.1 %shard_map.102 = (bf16[16,512]{1,0:T(8,128)(2,1)}, bf16[448,512]{1,0:T(8,128)(2,1)}, bf16[448,512]{1,0:T(8,128)(2,1)}, bf16[448,512]{1,0:T(8,128)(2,1)}) custom-call(f32[128,512]{1,0:T(8,128)} %x_ref.1, f32[448,128]{1,0:T(8,128)} %bitcast.10, f32[448,128]{1,0:T(8,128)} %bitcast.11, bf16[128,512]{1,0:T(8,128)(2,1)} %go_ref.1, bf16[448,512]{1,0:T(8,128)(2,1)} %bitcast.8, ...), custom_call_target="tpu_custom_call" | custom-call | tf_op jit(solution)/shard_map/pallas_call | solution.py:357
  116.8 1.3 %copy.15 = bf16[16,512]{1,0:T(8,128)(2,1)} copy(bf16[16,512]{1,0:T(8,128)(2,1)} %get-tuple-element.16) | data formatting | bytes 32768
  118.1 0.0 copy-start.1
  118.1 1.9 %copy.16 = bf16[512,448]{0,1:T(8,128)(2,1)} copy(bf16[512,448]{0,1:T(8,128)(2,1)} %bitcast.7) | data formatting | bytes 917504
  120.0 0.0 copy-done.1
  120.0 0.0 copy-start
  120.0 0.8 copy.17
  120.7 0.4 copy-done
  121.1 0.8 copy.18
Async XLA Ops:
  118.1 1.9 %copy-start.1 = (bf16[448,512]{1,0:T(8,128)(2,1)S(1)}, bf16[448,512]{1,0:T(8,128)(2,1)}, u32[]{:S(2)}) copy-start(bf16[448,512]{1,0:T(8,128)(2,1)} %get-tuple-element.10) | copy-start | bytes 1376260
  120.0 1.2 copy-start

commit v3 on v2

v3 whole, which is shorter than its diff:
```python
import functools

import jax
import jax.numpy as jnp
from jax import lax
from jax.experimental import pallas as pl
from jax.experimental.pallas import tpu as pltpu
from jax.sharding import PartitionSpec as P

MESH = pl.DeviceIdType.MESH
F32 = jnp.float32
BF16 = jnp.bfloat16
LAST = (((1,), (1,)), ((), ()))
LEAD = (((0,), (0,)), ((), ()))
NC = 2
NZ = 2
CH = 4
TP = 2
XM, XE = 3, 5
E0 = 3


def dot(a, b, dims=(((1,), (0,)), ((), ()))):
    return lax.dot_general(a, b, dims, preferred_element_type=F32)


def kernel(
    sizes,
    x_in, g_in, u_in, go_in, wg_in, wu_in, wd_in,
    ig_ref, gw_out, uw_out, dw_out,
    XF, GF, UF, WG, WU, WD,
    GA, XA, GU, H, RU, RD, PU, PD, PO, TA, TB, HD, GW, UW, DW, GO, UO, DO, FR,
    IG2, IGR, XS, XB, XR, YS, YR, ZR,
    in_s, out_s, ga_s, ga_r, xa_s, xa_r, gu_s, gu_r, h_s, h_r, ru_s, ru_r, rd_s, rd_r, fr_s, fr_r,
    ig_s, ig_r, xs_s, xs_r, ys_s, ys_r, z_s, z_r,
):
    NI, NO, NT = sizes
    NX, NY = NT // NC, NO // NZ
    zi, o, t = lax.axis_index("inp"), lax.axis_index("out"), lax.axis_index("tok")
    x, core = t // NC, t % NC
    y, zh = o // NZ, o % NZ
    F, tb = g_in.shape
    ts, D = go_in.shape
    fc = F // CH
    rows = tb // NT

    def at_inp(k):
        return {"inp": k}

    def at_tok(k):
        return {"tok": k}

    def at_out(k):
        return {"out": k}

    def rc(src, dst, ss, rs, dev):
        return pltpu.make_async_remote_copy(
            src_ref=src, dst_ref=dst, send_sem=ss, recv_sem=rs, device_id=dev, device_id_type=MESH
        )

    has_up, has_dn = zi < NI - 1, zi > 0
    sib = x * NC + (1 - core)

    def tok_of(dx):
        return ((x + dx + NX) % NX) * NC + core

    def rows_of(buf, k):
        return buf.at[pl.ds(pl.multiple_of(k * ts, ts), ts)]

    loads = [
        pltpu.make_async_copy(src, dst, in_s.at[i])
        for i, (src, dst) in enumerate(
            [(go_in, rows_of(GA, t)), (g_in, GF), (u_in, UF), (x_in, XF), (wd_in, WD), (wg_in, WG), (wu_in, WU)]
        )
    ]
    for c in loads:
        c.start()

    barrier = pltpu.get_barrier_semaphore()

    def greet(dev):
        pl.semaphore_signal(barrier, inc=1, device_id=dev, device_id_type=MESH)

    greet(at_tok(sib))
    for dx in range(1, NX):
        greet(at_tok(tok_of(dx)))
    for dy in range(1, NY):
        greet(at_out(((y + dy) % NY) * NZ + zh))
    greet(at_out(y * NZ + 1 - zh))
    pl.when(has_up)(lambda: greet(at_inp(zi + 1)))
    pl.when(has_dn)(lambda: greet(at_inp(zi - 1)))
    ends = jnp.where(has_up, 1, 0) + jnp.where(has_dn, 1, 0)
    pl.semaphore_wait(barrier, 1 + (NX - 1) + (NY - 1) + 1 + ends)

    def gather_tok(buf, ss, rs, pieces):
        step = ts // pieces

        def copy(k, slot, dev, c):
            part = buf.at[pl.ds(pl.multiple_of(k * ts + c * step, step), step)]
            return rc(part, part, ss.at[slot, c], rs.at[k, c], dev)

        near = [1, -1][: min(NX - 1, 2)]

        def sends():
            yield 0, (t, 0, at_tok(sib))
            for i, dx in enumerate(near):
                yield 0, (t, 1 + i, at_tok(tok_of(dx)))
            for i, dx in enumerate(near):
                yield 1, (tok_of(dx), 3 + i, at_tok(sib))
            if NX > 2:
                yield 1, (tok_of(2 * core - 1), 5, at_tok(tok_of(1 - 2 * core)))
                yield 2, (tok_of(2), 6, at_tok(sib))

        def arrived(k, c):
            copy(k, 0, at_tok(sib), c).wait_recv()

        def start(stage, c):
            for at, args in sends():
                if at == stage:
                    copy(*args, c).start()

        def begin():
            for c in range(pieces):
                start(0, c)

        def middle():
            for c in range(pieces):
                for dx in near:
                    arrived(tok_of(dx), c)
                start(1, c)

        def end():
            for c in range(pieces):
                if NX > 2:
                    arrived(tok_of(2), c)
                    start(2, c)
            for c in range(pieces):
                for dx in range(NX):
                    arrived(((x + dx) % NX) * NC + 1 - core, c)

        def drain():
            for c in range(pieces):
                for _, args in sends():
                    copy(*args, c).wait_send()

        return begin, middle, end, drain

    def hand(buf, ss, rs, j, c, up):
        return rc(buf.at[j, c], buf.at[j, c], ss.at[up, j, c], rs.at[j, c], at_inp(zi + 1 if up else zi - 1))

    def own_both(buf, ss, rs, c):
        pl.when(has_up)(lambda: hand(buf, ss, rs, zi, c, 1).start())
        pl.when(has_dn)(lambda: hand(buf, ss, rs, zi, c, 0).start())

    def pass_on(buf, ss, rs, s, c):
        @pl.when(zi + s <= NI - 1)
        def _():
            hand(buf, ss, rs, zi + s, c, 1).wait_recv()
            pl.when(has_dn)(lambda: hand(buf, ss, rs, zi + s, c, 0).start())

        @pl.when(zi - s >= 0)
        def _():
            hand(buf, ss, rs, zi - s, c, 0).wait_recv()
            pl.when(has_up)(lambda: hand(buf, ss, rs, zi - s, c, 1).start())

    def drain_z(buf, ss, rs, pieces):
        def body(j, carry):
            for c in range(pieces):
                pl.when(jnp.logical_and(has_up, j <= zi))(lambda c=c: hand(buf, ss, rs, j, c, 1).wait_send())
                pl.when(jnp.logical_and(has_dn, j >= zi))(lambda c=c: hand(buf, ss, rs, j, c, 0).wait_send())
            return carry

        lax.fori_loop(0, NI, body, 0)

    def order(n):
        m = jnp.minimum(zi, NI - 1 - zi)
        half = (n + 1) // 2
        near = jnp.where(n % 2 == 1, zi + half, zi - half)
        far = jnp.where(zi <= m, n, NI - 1 - n)
        return jnp.where(n <= 2 * m, near, far)

    def block(buf, j):
        return buf[pl.ds(pl.multiple_of(j * tb, tb), tb), :]

    def chain(buf, ss, rs, d, c, up):
        return rc(buf.at[d, c], buf.at[d, c], ss.at[d, c], rs.at[d, c], at_inp(zi + 1 if up else zi - 1))

    def up_on(k):
        return jnp.logical_and(zi <= k, has_up)

    def dn_on(k):
        return jnp.logical_and(k >= NI - 1 - zi, has_dn)

    def up_dst(k):
        return NI - 1 - k + zi

    def dn_dst(k):
        return k - (NI - 1 - zi)

    def products(k):
        @pl.when(up_on(k))
        def _():
            PU[...] = dot(WD[...], block(GA, up_dst(k)), LAST)

        @pl.when(dn_on(k))
        def _():
            PD[...] = dot(WD[...], block(GA, dn_dst(k)), LAST)

    def slot(k):
        for c in range(CH):
            piece = slice(c * fc, (c + 1) * fc)

            @pl.when(up_on(k))
            def _():
                d = up_dst(k)

                @pl.when(has_dn)
                def _():
                    chain(RU, ru_s, ru_r, d, c, 1).wait_recv()
                    RU[d, c] = (PU[piece, :] + RU[d, c].astype(F32)).astype(BF16)

                @pl.when(jnp.logical_not(has_dn))
                def _():
                    RU[d, c] = PU[piece, :].astype(BF16)

                chain(RU, ru_s, ru_r, d, c, 1).start()

            @pl.when(dn_on(k))
            def _():
                d = dn_dst(k)

                @pl.when(has_up)
                def _():
                    chain(RD, rd_s, rd_r, d, c, 0).wait_recv()
                    RD[d, c] = (PD[piece, :] + RD[d, c].astype(F32)).astype(BF16)

                @pl.when(jnp.logical_not(has_up))
                def _():
                    RD[d, c] = PD[piece, :].astype(BF16)

                chain(RD, rd_s, rd_r, d, c, 0).start()

    def last_hop(c, up):
        src = (PU if up else PD).at[pl.ds(c * fc, fc)]
        return rc(src, FR.at[up, c], fr_s.at[up, c], fr_r.at[up, c], at_inp(zi + 1 if up else zi - 1))

    def last_slot():
        for c in range(CH):
            piece = slice(c * fc, (c + 1) * fc)

            @pl.when(has_up)
            def _():
                @pl.when(has_dn)
                def _():
                    chain(RU, ru_s, ru_r, zi + 1, c, 1).wait_recv()
                    PU[piece, :] += RU[zi + 1, c].astype(F32)

                last_hop(c, 1).start()

            @pl.when(has_dn)
            def _():
                @pl.when(has_up)
                def _():
                    chain(RD, rd_s, rd_r, zi - 1, c, 0).wait_recv()
                    PD[piece, :] += RD[zi - 1, c].astype(F32)

                last_hop(c, 0).start()

    def close_chains(c):
        piece = slice(c * fc, (c + 1) * fc)

        @pl.when(has_dn)
        def _():
            last_hop(c, 1).wait_recv()
            PO[piece, :] += FR[1, c]

        @pl.when(has_up)
        def _():
            last_hop(c, 0).wait_recv()
            PO[piece, :] += FR[0, c]

        H[zi, c] = PO[piece, :].astype(BF16)

    def drain_chains():
        def body(d, carry):
            for c in range(CH):
                pl.when(d > zi + 1)(lambda c=c: chain(RU, ru_s, ru_r, d, c, 1).wait_send())
                pl.when(d < zi - 1)(lambda c=c: chain(RD, rd_s, rd_r, d, c, 0).wait_send())
            return carry

        lax.fori_loop(0, NI, body, 0)
        for c in range(CH):
            pl.when(has_up)(lambda c=c: last_hop(c, 1).wait_send())
            pl.when(has_dn)(lambda c=c: last_hop(c, 0).wait_send())

    def terms(n):
        j = order(n)
        g, u = GU[j, 0].astype(F32), GU[j, 1].astype(F32)
        sig = 1.0 / (1.0 + jnp.exp(-g))
        gs = g * sig
        TA[n] = u * sig * (1.0 + g * (1.0 - sig))
        TB[n] = gs
        HD[n] = (gs * u).astype(BF16)

    def grads(n):
        j = order(n)
        h = H[j].reshape(F, tb).astype(F32)
        gg, ug = (h * TA[n]).astype(BF16), (h * TB[n]).astype(BF16)
        part = dot(gg, WG[...], LEAD) + dot(ug, WU[...], LEAD)
        part = part.reshape(NX, NC, rows, D)
        for c in range(NC):
            IG2[c, n] = part[:, c]
        ig_core(n).start()
        xb = block(XA, j)
        GW[...] += dot(gg, xb)
        UW[...] += dot(ug, xb)
        DW[...] += dot(HD[n], block(GA, j))

    def ig_core(n):
        return rc(IG2.at[1 - core, n], IGR.at[n], ig_s.at[n], ig_r.at[n], at_tok(sib))

    def ig_x(n, dx):
        return rc(
            XB.at[n, (x + dx) % NX], XR.at[dx - 1, n], xs_s.at[dx - 1, n], xs_r.at[dx - 1, n], at_tok(tok_of(dx))
        )

    def ig_y(n):
        j = order(n)
        root = j // NZ
        far = (y - root + NY) % NY - 1
        return rc(YS.at[j], YR.at[far, j % NZ], ys_s.at[n], ys_r.at[far, j % NZ], at_out(root * NZ + zh))

    def ig_z():
        j = y * NZ + 1 - zh
        return rc(YS.at[j], ZR, z_s, z_r, at_out(j))

    def sum_core(n):
        ig_core(n).wait()
        XS[n] = IG2[core, n] + IGR[n]
        XB[n] = XS[n].astype(BF16)
        for dx in range(1, NX):
            ig_x(n, dx).start()

    def sum_x(n):
        total = XS[n, x]
        for dx in range(1, NX):
            ig_x(n, dx).wait()
            total = total + XR[dx - 1, n].astype(F32)
        YS[order(n)] = total
        pl.when(y != order(n) // NZ)(lambda: ig_y(n).start())

    def sum_y(n):
        j = order(n)

        @pl.when(y != j // NZ)
        def _():
            ig_y(n).wait_send()

        @pl.when(y == j // NZ)
        def _():
            total = YS[j]
            for far in range(NY - 1):
                rc(YS.at[j], YR.at[far, j % NZ], ys_s.at[n], ys_r.at[far, j % NZ], at_out(y * NZ + 1 - zh)).wait_recv()
                total = total + YR[far, j % NZ]
            YS[j] = total
            pl.when(zh != j % NZ)(lambda: ig_z().start())

    loads[0].wait()
    g_begin, g_middle, g_end, g_drain = gather_tok(GA, ga_s, ga_r, TP)
    g_begin()
    loads[1].wait()
    GU[zi, 0] = GF[...].astype(BF16)
    own_both(GU, gu_s, gu_r, 0)
    loads[2].wait()
    GU[zi, 1] = UF[...].astype(BF16)
    own_both(GU, gu_s, gu_r, 1)
    loads[3].wait()
    XA[pl.ds(pl.multiple_of(t * ts, ts), ts), :] = XF[...].astype(BF16)
    x_begin, x_middle, x_end, x_drain = gather_tok(XA, xa_s, xa_r, TP)

    def gu_event(e):
        pl.when(e < 2 * (NI - 1))(lambda: pass_on(GU, gu_s, gu_r, e // 2 + 1, e % 2))

    GW[...] = jnp.zeros_like(GW)
    UW[...] = jnp.zeros_like(UW)
    DW[...] = jnp.zeros_like(DW)
    for c in loads[4:]:
        c.wait()
    g_middle()
    x_begin()
    for e in range(E0):
        gu_event(e)
    g_end()
    products(0)

    def rs_step(k, carry):
        slot(k)
        gu_event(E0 + k)
        products(k + 1)
        pl.when(k == XM)(x_middle)
        pl.when(k == XE)(x_end)
        pl.when(k >= 2)(lambda: terms(k - 2))
        return carry

    lax.fori_loop(0, NI - 2, rs_step, 0)
    last_slot()
    gu_event(E0 + NI - 2)
    if XM > NI - 3:
        x_middle()
    if XE > NI - 3:
        x_end()
    first_terms = max(NI - 4, 0)
    PO[...] = dot(WD[...], block(GA, zi), LAST)
    for c in range(CH):
        close_chains(c)
        own_both(H, h_s, h_r, c)
    events = E0 + NI - 1

    def h_step(s, carry):
        for c in range(CH):
            pass_on(H, h_s, h_r, s, c)
            if c == 0:
                gu_event(events + s - 1)
        for n in range(first_terms, NI):
            pl.when(s == max(n - first_terms, 2 * n - events, 1))(lambda n=n: terms(n))
        pl.when(s == 1)(lambda: grads(0))
        grads(s)
        sum_core(s - 1)
        pl.when(s >= 2)(lambda: sum_x(s - 2))
        pl.when(s >= 3)(lambda: sum_y(s - 3))
        return carry

    lax.fori_loop(1, NI, h_step, 0)
    sum_core(NI - 1)
    outs = []
    for i, (acc, stage, out) in enumerate([(GW, GO, gw_out), (UW, UO, uw_out), (DW, DO, dw_out)]):
        if i == 1:
            sum_x(NI - 2)
            sum_x(NI - 1)
        stage[...] = acc[...].astype(BF16)
        outs.append(pltpu.make_async_copy(stage, out, out_s.at[i]))
        outs[-1].start()
    for n in range(max(NI - 3, 0), NI):
        sum_y(n)
    g_drain()
    x_drain()
    drain_z(GU, gu_s, gu_r, 2)
    drain_z(H, h_s, h_r, CH)
    drain_chains()
    ig_z().wait()
    ig_ref[...] = (YS[o] + ZR[...]).astype(BF16)
    for c in outs:
        c.wait()


def copy_out(*refs):
    n = (len(refs) - 2) // 3
    ins, outs, held, (in_s, out_s) = refs[:n], refs[n : 2 * n], refs[2 * n : 3 * n], refs[3 * n :]
    first = [pltpu.make_async_copy(ins[i], held[i], in_s.at[i]) for i in range(n)]
    second = [pltpu.make_async_copy(held[i], outs[i], out_s.at[i]) for i in range(n)]
    for c in first:
        c.start()
    for c, d in zip(first, second):
        c.wait()
        d.start()
    for d in second:
        d.wait()


def local(saved_input, saved_gate, saved_up, out_grad, w_gate, w_up, w_down):
    sizes = tuple(lax.axis_size(a) for a in ("inp", "out", "tok"))
    NI, NO, NT = sizes
    NX, NY = NT // NC, NO // NZ
    ts, D = saved_input.shape
    tb, F = saved_gate.shape
    T = tb * NI
    rows = tb // NT
    dma = pltpu.SemaphoreType.DMA
    vmem = pl.BlockSpec(memory_space=pltpu.VMEM)
    anyw = pl.BlockSpec(memory_space=pl.ANY)
    fc = F // CH
    ig, gw, uw, dw = pl.pallas_call(
        functools.partial(kernel, sizes),
        out_shape=(
            jax.ShapeDtypeStruct((rows, D), BF16),
            jax.ShapeDtypeStruct((F, D), BF16),
            jax.ShapeDtypeStruct((F, D), BF16),
            jax.ShapeDtypeStruct((F, D), BF16),
        ),
        in_specs=[anyw] * 7,
        out_specs=(vmem, anyw, anyw, anyw),
        scratch_shapes=[
            pltpu.VMEM((ts, D), F32),
            pltpu.VMEM((F, tb), F32),
            pltpu.VMEM((F, tb), F32),
            pltpu.VMEM((F, D), BF16),
            pltpu.VMEM((F, D), BF16),
            pltpu.VMEM((F, D), BF16),
            pltpu.VMEM((T, D), BF16),
            pltpu.VMEM((T, D), BF16),
            pltpu.VMEM((NI, 2, F, tb), BF16),
            pltpu.VMEM((NI, CH, fc, tb), BF16),
            pltpu.VMEM((NI, CH, fc, tb), BF16),
            pltpu.VMEM((NI, CH, fc, tb), BF16),
            pltpu.VMEM((F, tb), F32),
            pltpu.VMEM((F, tb), F32),
            pltpu.VMEM((F, tb), F32),
            pltpu.VMEM((NI, F, tb), F32),
            pltpu.VMEM((NI, F, tb), F32),
            pltpu.VMEM((NI, F, tb), BF16),
            pltpu.VMEM((F, D), F32),
            pltpu.VMEM((F, D), F32),
            pltpu.VMEM((F, D), F32),
            pltpu.VMEM((F, D), BF16),
            pltpu.VMEM((F, D), BF16),
            pltpu.VMEM((F, D), BF16),
            pltpu.VMEM((2, CH, fc, tb), F32),
            pltpu.VMEM((NC, NI, NX, rows, D), F32),
            pltpu.VMEM((NI, NX, rows, D), F32),
            pltpu.VMEM((NI, NX, rows, D), F32),
            pltpu.VMEM((NI, NX, rows, D), BF16),
            pltpu.VMEM((max(NX - 1, 1), NI, rows, D), BF16),
            pltpu.VMEM((NO, rows, D), F32),
            pltpu.VMEM((max(NY - 1, 1), NZ, rows, D), F32),
            pltpu.VMEM((rows, D), F32),
            dma((7,)), dma((3,)),
            dma((7, TP)), dma((NT, TP)), dma((7, TP)), dma((NT, TP)),
            dma((2, NI, 2)), dma((NI, 2)), dma((2, NI, CH)), dma((NI, CH)),
            dma((NI, CH)), dma((NI, CH)), dma((NI, CH)), dma((NI, CH)), dma((2, CH)), dma((2, CH)),
            dma((NI,)), dma((NI,)),
            dma((max(NX - 1, 1), NI)), dma((max(NX - 1, 1), NI)),
            dma((NI,)), dma((max(NY - 1, 1), NZ)), dma, dma,
        ],
        compiler_params=pltpu.CompilerParams(
            collective_id=0, has_side_effects=True, vmem_limit_bytes=56 * 1024 * 1024
        ),
    )(saved_input, saved_gate.T, saved_up.T, out_grad, w_gate.T, w_up.T, w_down)
    results = (ig, gw, uw, dw)
    ig, gw, uw, dw = pl.pallas_call(
        copy_out,
        out_shape=tuple(jax.ShapeDtypeStruct(r.shape, r.dtype) for r in results),
        in_specs=[anyw] * 4,
        out_specs=(anyw,) * 4,
        scratch_shapes=[pltpu.VMEM(r.shape, r.dtype) for r in results] + [dma((4,)), dma((4,))],
    )(*results)
    return ig, gw.T, uw.T, dw


def solution(mesh):
    placed = (
        P("tok", "inp"),
        P("inp", ("out", "tok")),
        P("inp", ("out", "tok")),
        P("tok", "inp"),
        P("inp", ("out", "tok")),
        P("inp", ("out", "tok")),
        P(("out", "tok"), "inp"),
    )
    return jax.shard_map(
        local,
        mesh=mesh,
        in_specs=placed,
        out_specs=(
            P(("out", "tok"), "inp"),
            P("inp", ("out", "tok")),
            P("inp", ("out", "tok")),
            P(("out", "tok"), "inp"),
        ),
        check_vma=False,
    )
```

time: 124 us -> 101 us (0.81); the launches traced: 122 us -> 101 us
  Pallas kernels: 116 us -> 99.9 us
  local copies, waits for them, and re-layouts: 5.15 us -> 0 us
    pallas_call x1, Pallas kernels: 116 us -> 97.7 us  [local(): pl.pallas_call(functools.partial(kernel, sizes), out_shape=(jax.ShapeDtyp...]
    unnamed x8 -> x0, local copies, waits for them, and re-layouts: 5.15 us -> none
    pallas_call x0 -> x1, Pallas kernels: none -> 2.17 us  [local(): pl.pallas_call(copy_out, out_shape=tuple((jax.ShapeDtypeStruct(r.shape, r...]
where the time goes in v3:
time: 101 us
  Pallas kernels  99.9 us (99%)
    pallas_call x1, Pallas kernels, local(): pl.pallas_call(functools.partial(kernel, sizes), out_shape=(jax.ShapeDtyp...  97.7 us
    pallas_call x1, Pallas kernels, local(): pl.pallas_call(copy_out, out_shape=tuple((jax.ShapeDtypeStruct(r.shape, r...  2.17 us

profile of v3, /device:TPU:24, one launch (start us, length us, event | category | flops | bytes accessed | tf_op | source)
XLA Modules:
  0.0 100.5 jit_solution(14262114395503278005)
XLA Ops:
  0.6 97.7 %shard_map.102 = (bf16[16,512]{1,0:T(8,128)(2,1)}, bf16[448,512]{1,0:T(8,128)(2,1)}, bf16[448,512]{1,0:T(8,128)(2,1)}, bf16[448,512]{1,0:T(8,128)(2,1)}) custom-call(f32[128,512]{1,0:T(8,128)} %x_in.1, f32[448,128]{1,0:T(8,128)} %bitcast.8, f32[448,128]{1,0:T(8,128)} %bitcast.9, bf16[128,512]{1,0:T(8,128)(2,1)} %go_in.1, bf16[448,512]{1,0:T(8,128)(2,1)} %bitcast.6, ...), custom_call_target="tpu_custom_call" | custom-call | tf_op jit(solution)/shard_map/pallas_call | solution.py:482
  98.3 2.2 %shard_map.103 = (bf16[16,512]{1,0:T(8,128)(2,1)}, bf16[448,512]{1,0:T(8,128)(2,1)}, bf16[448,512]{1,0:T(8,128)(2,1)}, bf16[448,512]{1,0:T(8,128)(2,1)}) custom-call(bf16[16,512]{1,0:T(8,128)(2,1)} %get-tuple-element.12.refs_0_, bf16[448,512]{1,0:T(8,128)(2,1)} %get-tuple-element.13.refs_1_, bf16[448,512]{1,0:T(8,128)(2,1)} %get-tuple-element.14.refs_2_, ...), custom_call_target="tpu_custom_call" | custom-call | tf_op jit(solution)/shard_map/pallas_call | solution.py:539

commit v4 on v3

--- a/solution.py
+++ b/solution.py
@@ -17,6 +17,8 @@
 CH = 4
 TP = 2
 XM, XE = 3, 5
+LAST_HOP = BF16
+Z_HOP = BF16
 E0 = 3
 
 
@@ -29,9 +31,9 @@
     x_in, g_in, u_in, go_in, wg_in, wu_in, wd_in,
     ig_ref, gw_out, uw_out, dw_out,
     XF, GF, UF, WG, WU, WD,
-    GA, XA, GU, H, RU, RD, PU, PD, PO, TA, TB, HD, GW, UW, DW, GO, UO, DO, FR,
-    IG2, IGR, XS, XB, XR, YS, YR, ZR,
-    in_s, out_s, ga_s, ga_r, xa_s, xa_r, gu_s, gu_r, h_s, h_r, ru_s, ru_r, rd_s, rd_r, fr_s, fr_r,
+    GA, XA, GU, H, RU, RD, PU, PD, PO, TA, TB, HD, GW, UW, DW, FS, FR,
+    IG2, IGR, XS, XB, XR, YS, YR, ZS, ZR,
+    in_s, ga_s, ga_r, xa_s, xa_r, gu_s, gu_r, h_s, h_r, ru_s, ru_r, rd_s, rd_r, fr_s, fr_r,
     ig_s, ig_r, xs_s, xs_r, ys_s, ys_r, z_s, z_r,
 ):
     NI, NO, NT = sizes
@@ -241,8 +243,7 @@
                 chain(RD, rd_s, rd_r, d, c, 0).start()
 
     def last_hop(c, up):
-        src = (PU if up else PD).at[pl.ds(c * fc, fc)]
-        return rc(src, FR.at[up, c], fr_s.at[up, c], fr_r.at[up, c], at_inp(zi + 1 if up else zi - 1))
+        return rc(FS.at[up, c], FR.at[up, c], fr_s.at[up, c], fr_r.at[up, c], at_inp(zi + 1 if up else zi - 1))
 
     def last_slot():
         for c in range(CH):
@@ -255,6 +256,7 @@
                     chain(RU, ru_s, ru_r, zi + 1, c, 1).wait_recv()
                     PU[piece, :] += RU[zi + 1, c].astype(F32)
 
+                FS[1, c] = PU[piece, :].astype(FS.dtype)
                 last_hop(c, 1).start()
 
             @pl.when(has_dn)
@@ -264,6 +266,7 @@
                     chain(RD, rd_s, rd_r, zi - 1, c, 0).wait_recv()
                     PD[piece, :] += RD[zi - 1, c].astype(F32)
 
+                FS[0, c] = PD[piece, :].astype(FS.dtype)
                 last_hop(c, 0).start()
 
     def close_chains(c):
@@ -272,12 +275,12 @@
         @pl.when(has_dn)
         def _():
             last_hop(c, 1).wait_recv()
-            PO[piece, :] += FR[1, c]
+            PO[piece, :] += FR[1, c].astype(F32)
 
         @pl.when(has_up)
         def _():
             last_hop(c, 0).wait_recv()
-            PO[piece, :] += FR[0, c]
+            PO[piece, :] += FR[0, c].astype(F32)
 
         H[zi, c] = PO[piece, :].astype(BF16)
 
@@ -332,7 +335,7 @@
 
     def ig_z():
         j = y * NZ + 1 - zh
-        return rc(YS.at[j], ZR, z_s, z_r, at_out(j))
+        return rc(ZS, ZR, z_s, z_r, at_out(j))
 
     def sum_core(n):
         ig_core(n).wait()
@@ -363,7 +366,11 @@
                 rc(YS.at[j], YR.at[far, j % NZ], ys_s.at[n], ys_r.at[far, j % NZ], at_out(y * NZ + 1 - zh)).wait_recv()
                 total = total + YR[far, j % NZ]
             YS[j] = total
-            pl.when(zh != j % NZ)(lambda: ig_z().start())
+
+            @pl.when(zh != j % NZ)
+            def _():
+                ZS[...] = total.astype(ZS.dtype)
+                ig_z().start()
 
     loads[0].wait()
     g_begin, g_middle, g_end, g_drain = gather_tok(GA, ga_s, ga_r, TP)
@@ -432,39 +439,29 @@
 
     lax.fori_loop(1, NI, h_step, 0)
     sum_core(NI - 1)
-    outs = []
-    for i, (acc, stage, out) in enumerate([(GW, GO, gw_out), (UW, UO, uw_out), (DW, DO, dw_out)]):
-        if i == 1:
-            sum_x(NI - 2)
-            sum_x(NI - 1)
-        stage[...] = acc[...].astype(BF16)
-        outs.append(pltpu.make_async_copy(stage, out, out_s.at[i]))
-        outs[-1].start()
+    gw_out[...] = GW[...].astype(BF16)
+    sum_x(NI - 2)
+    sum_x(NI - 1)
+    uw_out[...] = UW[...].astype(BF16)
     for n in range(max(NI - 3, 0), NI):
         sum_y(n)
+    dw_out[...] = DW[...].astype(BF16)
     g_drain()
     x_drain()
     drain_z(GU, gu_s, gu_r, 2)
     drain_z(H, h_s, h_r, CH)
     drain_chains()
     ig_z().wait()
-    ig_ref[...] = (YS[o] + ZR[...]).astype(BF16)
-    for c in outs:
+    ig_ref[...] = (YS[o] + ZR[...].astype(F32)).astype(BF16)
+
+
+def copy_out(*refs):
+    n = len(refs) // 2
+    copies = [pltpu.make_async_copy(refs[i], refs[n + i], refs[-1].at[i]) for i in range(n)]
+    for c in copies:
+        c.start()
+    for c in copies:
         c.wait()
-
-
-def copy_out(*refs):
-    n = (len(refs) - 2) // 3
-    ins, outs, held, (in_s, out_s) = refs[:n], refs[n : 2 * n], refs[2 * n : 3 * n], refs[3 * n :]
-    first = [pltpu.make_async_copy(ins[i], held[i], in_s.at[i]) for i in range(n)]
-    second = [pltpu.make_async_copy(held[i], outs[i], out_s.at[i]) for i in range(n)]
-    for c in first:
-        c.start()
-    for c, d in zip(first, second):
-        c.wait()
-        d.start()
-    for d in second:
-        d.wait()
 
 
 def local(saved_input, saved_gate, saved_up, out_grad, w_gate, w_up, w_down):
@@ -482,13 +479,13 @@
     ig, gw, uw, dw = pl.pallas_call(
         functools.partial(kernel, sizes),
         out_shape=(
-            jax.ShapeDtypeStruct((rows, D), BF16),
-            jax.ShapeDtypeStruct((F, D), BF16),
-            jax.ShapeDtypeStruct((F, D), BF16),
-            jax.ShapeDtypeStruct((F, D), BF16),
+            pltpu.VMEM((rows, D), BF16),
+            pltpu.VMEM((F, D), BF16),
+            pltpu.VMEM((F, D), BF16),
+            pltpu.VMEM((F, D), BF16),
         ),
         in_specs=[anyw] * 7,
-        out_specs=(vmem, anyw, anyw, anyw),
+        out_specs=(vmem,) * 4,
         scratch_shapes=[
             pltpu.VMEM((ts, D), F32),
             pltpu.VMEM((F, tb), F32),
@@ -511,10 +508,8 @@
             pltpu.VMEM((F, D), F32),
             pltpu.VMEM((F, D), F32),
             pltpu.VMEM((F, D), F32),
-            pltpu.VMEM((F, D), BF16),
-            pltpu.VMEM((F, D), BF16),
-            pltpu.VMEM((F, D), BF16),
-            pltpu.VMEM((2, CH, fc, tb), F32),
+            pltpu.VMEM((2, CH, fc, tb), LAST_HOP),
+            pltpu.VMEM((2, CH, fc, tb), LAST_HOP),
             pltpu.VMEM((NC, NI, NX, rows, D), F32),
             pltpu.VMEM((NI, NX, rows, D), F32),
             pltpu.VMEM((NI, NX, rows, D), F32),
@@ -522,8 +517,9 @@
             pltpu.VMEM((max(NX - 1, 1), NI, rows, D), BF16),
             pltpu.VMEM((NO, rows, D), F32),
             pltpu.VMEM((max(NY - 1, 1), NZ, rows, D), F32),
-            pltpu.VMEM((rows, D), F32),
-            dma((7,)), dma((3,)),
+            pltpu.VMEM((rows, D), Z_HOP),
+            pltpu.VMEM((rows, D), Z_HOP),
+            dma((7,)),
             dma((7, TP)), dma((NT, TP)), dma((7, TP)), dma((NT, TP)),
             dma((2, NI, 2)), dma((NI, 2)), dma((2, NI, CH)), dma((NI, CH)),
             dma((NI, CH)), dma((NI, CH)), dma((NI, CH)), dma((NI, CH)), dma((2, CH)), dma((2, CH)),
@@ -539,10 +535,10 @@
     ig, gw, uw, dw = pl.pallas_call(
         copy_out,
         out_shape=tuple(jax.ShapeDtypeStruct(r.shape, r.dtype) for r in results),
-        in_specs=[anyw] * 4,
+        in_specs=[vmem] * 4,
         out_specs=(anyw,) * 4,
-        scratch_shapes=[pltpu.VMEM(r.shape, r.dtype) for r in results] + [dma((4,)), dma((4,))],
-    )(*results)
+        scratch_shapes=[dma((4,))],
+    )(*[pltpu.with_memory_space_constraint(r, pltpu.VMEM) for r in results])
     return ig, gw.T, uw.T, dw
 
 

time: 101 us -> 96.4 us (0.954)
  Pallas kernels: 99.9 us -> 95.6 us
    pallas_call x1, Pallas kernels: 97.7 us -> 94.5 us  [local(): pl.pallas_call(functools.partial(kernel, sizes), out_shape=(pltpu.VMEM((r...]
    pallas_call x1, Pallas kernels: 2.17 us -> 1.11 us  [local(): pl.pallas_call(copy_out, out_shape=tuple((jax.ShapeDtypeStruct(r.shape, r...]
where the time goes in v4:
time: 96.4 us; the launch traced here: 96.3 us
  Pallas kernels  95.6 us (99%)
    pallas_call x1, Pallas kernels, local(): pl.pallas_call(functools.partial(kernel, sizes), out_shape=(pltpu.VMEM((r...  94.5 us

profile of v4, /device:TPU:24, one launch (start us, length us, event | category | flops | bytes accessed | tf_op | source)
XLA Modules:
  0.0 96.3 jit_solution(6704906335751467777)
XLA Ops:
  0.6 94.5 %shard_map.102 = (bf16[16,512]{1,0:T(8,128)(2,1)S(1)}, bf16[448,512]{1,0:T(8,128)(2,1)S(1)}, bf16[448,512]{1,0:T(8,128)(2,1)S(1)}, bf16[448,512]{1,0:T(8,128)(2,1)S(1)}) custom-call(f32[128,512]{1,0:T(8,128)} %x_in.1, f32[448,128]{1,0:T(8,128)} %bitcast.8, f32[448,128]{1,0:T(8,128)} %bitcast.9, bf16[128,512]{1,0:T(8,128)(2,1)} %go_in.1, ...), custom_call_target="tpu_custom_call" | custom-call | tf_op jit(solution)/shard_map/pallas_call | solution.py:479
  95.2 1.1 %shard_map.103 = (bf16[16,512]{1,0:T(8,128)(2,1)}, bf16[448,512]{1,0:T(8,128)(2,1)}, bf16[448,512]{1,0:T(8,128)(2,1)}, bf16[448,512]{1,0:T(8,128)(2,1)}) custom-call(bf16[16,512]{1,0:T(8,128)(2,1)S(1)} %get-tuple-element.12.refs_0_, bf16[448,512]{1,0:T(8,128)(2,1)S(1)} %get-tuple-element.13.refs_1_, bf16[448,512]{1,0:T(8,128)(2,1)S(1)} %get-tuple-element.14.refs_2_, ...), custom_call_target="tpu_custom_call" | custom-call | tf_op jit(solution)/shard_map/pallas_call | solution.py:535

commit v5 on v4

--- a/solution.py
+++ b/solution.py
@@ -15,11 +15,11 @@
 NC = 2
 NZ = 2
 CH = 4
-TP = 2
+TP = 1
 XM, XE = 3, 5
 LAST_HOP = BF16
-Z_HOP = BF16
-E0 = 3
+Z_HOP = F32
+E0 = 4
 
 
 def dot(a, b, dims=(((1,), (0,)), ((), ()))):
@@ -431,20 +431,22 @@
         for n in range(first_terms, NI):
             pl.when(s == max(n - first_terms, 2 * n - events, 1))(lambda n=n: terms(n))
         pl.when(s == 1)(lambda: grads(0))
-        grads(s)
         sum_core(s - 1)
         pl.when(s >= 2)(lambda: sum_x(s - 2))
         pl.when(s >= 3)(lambda: sum_y(s - 3))
+        grads(s)
         return carry
 
     lax.fori_loop(1, NI, h_step, 0)
     sum_core(NI - 1)
+    sum_x(NI - 2)
     gw_out[...] = GW[...].astype(BF16)
-    sum_x(NI - 2)
+    if NI > 2:
+        sum_y(NI - 3)
     sum_x(NI - 1)
+    sum_y(NI - 2)
     uw_out[...] = UW[...].astype(BF16)
-    for n in range(max(NI - 3, 0), NI):
-        sum_y(n)
+    sum_y(NI - 1)
     dw_out[...] = DW[...].astype(BF16)
     g_drain()
     x_drain()

time: 96.4 us -> 95.5 us (level)
  no operation moved by 1% of the time
where the time goes in v5:
time: 95.5 us; the launch traced here: 95.3 us
  Pallas kernels  94.7 us (99%)
    pallas_call x1, Pallas kernels, local(): pl.pallas_call(functools.partial(kernel, sizes), out_shape=(pltpu.VMEM((r...  93.6 us

profile of v5, /device:TPU:24, one launch (start us, length us, event | category | flops | bytes accessed | tf_op | source)
XLA Modules:
  0.0 95.3 jit_solution(2140402937541231278)
XLA Ops:
  0.6 93.6 %shard_map.102 = (bf16[16,512]{1,0:T(8,128)(2,1)S(1)}, bf16[448,512]{1,0:T(8,128)(2,1)S(1)}, bf16[448,512]{1,0:T(8,128)(2,1)S(1)}, bf16[448,512]{1,0:T(8,128)(2,1)S(1)}) custom-call(f32[128,512]{1,0:T(8,128)} %x_in.1, f32[448,128]{1,0:T(8,128)} %bitcast.8, f32[448,128]{1,0:T(8,128)} %bitcast.9, bf16[128,512]{1,0:T(8,128)(2,1)} %go_in.1, ...), custom_call_target="tpu_custom_call" | custom-call | tf_op jit(solution)/shard_map/pallas_call | solution.py:481
  94.2 1.1 %shard_map.103 = (bf16[16,512]{1,0:T(8,128)(2,1)}, bf16[448,512]{1,0:T(8,128)(2,1)}, bf16[448,512]{1,0:T(8,128)(2,1)}, bf16[448,512]{1,0:T(8,128)(2,1)}) custom-call(bf16[16,512]{1,0:T(8,128)(2,1)S(1)} %get-tuple-element.12.refs_0_, bf16[448,512]{1,0:T(8,128)(2,1)S(1)} %get-tuple-element.13.refs_1_, bf16[448,512]{1,0:T(8,128)(2,1)S(1)} %get-tuple-element.14.refs_2_, ...), custom_call_target="tpu_custom_call" | custom-call | tf_op jit(solution)/shard_map/pallas_call | solution.py:537

commit v6 on v5

--- a/solution.py
+++ b/solution.py
@@ -92,6 +92,13 @@
     pl.when(has_up)(lambda: greet(at_inp(zi + 1)))
     pl.when(has_dn)(lambda: greet(at_inp(zi - 1)))
     ends = jnp.where(has_up, 1, 0) + jnp.where(has_dn, 1, 0)
+    loads[1].wait()
+    GU[zi, 0] = GF[...].astype(BF16)
+    loads[2].wait()
+    GU[zi, 1] = UF[...].astype(BF16)
+    loads[3].wait()
+    XA[pl.ds(pl.multiple_of(t * ts, ts), ts), :] = XF[...].astype(BF16)
+    loads[0].wait()
     pl.semaphore_wait(barrier, 1 + (NX - 1) + (NY - 1) + 1 + ends)
 
     def gather_tok(buf, ss, rs, pieces):
@@ -372,17 +379,10 @@
                 ZS[...] = total.astype(ZS.dtype)
                 ig_z().start()
 
-    loads[0].wait()
     g_begin, g_middle, g_end, g_drain = gather_tok(GA, ga_s, ga_r, TP)
     g_begin()
-    loads[1].wait()
-    GU[zi, 0] = GF[...].astype(BF16)
     own_both(GU, gu_s, gu_r, 0)
-    loads[2].wait()
-    GU[zi, 1] = UF[...].astype(BF16)
     own_both(GU, gu_s, gu_r, 1)
-    loads[3].wait()
-    XA[pl.ds(pl.multiple_of(t * ts, ts), ts), :] = XF[...].astype(BF16)
     x_begin, x_middle, x_end, x_drain = gather_tok(XA, xa_s, xa_r, TP)
 
     def gu_event(e):

time: 95.5 us -> 95.5 us (level)
  no operation moved by 1% of the time
where the time goes in v6:
time: 95.5 us; the launch traced here: 95.3 us
  Pallas kernels  94.7 us (99%)
    pallas_call x1, Pallas kernels, local(): pl.pallas_call(functools.partial(kernel, sizes), out_shape=(pltpu.VMEM((r...  93.6 us

profile of v6, /device:TPU:24, one launch (start us, length us, event | category | flops | bytes accessed | tf_op | source)
XLA Modules:
  0.0 95.3 jit_solution(266120365570302448)
XLA Ops:
  0.6 93.6 %shard_map.102 = (bf16[16,512]{1,0:T(8,128)(2,1)S(1)}, bf16[448,512]{1,0:T(8,128)(2,1)S(1)}, bf16[448,512]{1,0:T(8,128)(2,1)S(1)}, bf16[448,512]{1,0:T(8,128)(2,1)S(1)}) custom-call(f32[128,512]{1,0:T(8,128)} %x_in.1, f32[448,128]{1,0:T(8,128)} %bitcast.8, f32[448,128]{1,0:T(8,128)} %bitcast.9, bf16[128,512]{1,0:T(8,128)(2,1)} %go_in.1, ...), custom_call_target="tpu_custom_call" | custom-call | tf_op jit(solution)/shard_map/pallas_call | solution.py:481
  94.2 1.1 %shard_map.103 = (bf16[16,512]{1,0:T(8,128)(2,1)}, bf16[448,512]{1,0:T(8,128)(2,1)}, bf16[448,512]{1,0:T(8,128)(2,1)}, bf16[448,512]{1,0:T(8,128)(2,1)}) custom-call(bf16[16,512]{1,0:T(8,128)(2,1)S(1)} %get-tuple-element.12.refs_0_, bf16[448,512]{1,0:T(8,128)(2,1)S(1)} %get-tuple-element.13.refs_1_, bf16[448,512]{1,0:T(8,128)(2,1)S(1)} %get-tuple-element.14.refs_2_, ...), custom_call_target="tpu_custom_call" | custom-call | tf_op jit(solution)/shard_map/pallas_call | solution.py:537
